TPU v7x, 32 devices: a whole 2x2x4 slice. The times are simulated.
32 devices in a mesh: node: 8 (over z, x), feat: 4 (over y, core).
Axes of the slice: x: 2, y: 2, z: 4, core: 2. Of those that a mesh axis runs over, the one named last changes fastest.
Arguments:
- features: bfloat16 [256, 4096], P('feat', 'node'), may hold values from -6 to 6
- tile_values: bfloat16 [256, 128, 128], P('node'), may hold values from -0.1875 to 0.1875
- tile_rows: int32 [64, 4], P('node'), may hold values from 0 to 3
- tile_cols: int32 [64, 4], P('node'), may hold values from 0 to 3
- tile_counts: int32 [64], P('node'), may hold values from 0 to 4, as said below
- weight: bfloat16 [256, 256], replicated, may hold values from -0.375 to 0.375
- cotangent: bfloat16 [256, 4096], P(None, ('node', 'feat')), may hold values from -6 to 6
Outputs:
- activated: bfloat16 [256, 4096], P(None, ('node', 'feat'))
- grad_weight: float32 [256, 256], replicated
- grad_features: float32 [256, 4096], P('feat', 'node')
Inputs may be any that keep to these rules, and one draw needn't show every extreme that they name: `tile_counts`: slots at or past a pair's count are ignored; some pair has all 4 slots live, and the live slots of one receiving node index vary strongly between indices.
All inputs are finite; a program needn't handle non-finite values.
Results may differ from a plain program's by a relative error of at most 0.012.
Values may be sent and summed in bfloat16 or wider, within the bound.
No kernel may reach another device: no remote copies, remote signals or barrier semaphores. Data moves between devices by JAX's collectives and lax.ppermute only.
A program may use at most 64 MiB of HBM per device.

v0:
```python
import jax
import jax.numpy as jnp
from jax import lax
from jax.sharding import PartitionSpec as P


def passed_along(x, axis, by):
    count = lax.axis_size(axis)
    return lax.ppermute(x, axis, [(i, (i + by) % count) for i in range(count)])


def select_pair(tile_values, tile_rows, tile_cols, tile_counts, source):
    slots = tile_rows.shape[1]
    values = lax.dynamic_slice_in_dim(tile_values, source * slots, slots, 0)
    row_ids = lax.dynamic_index_in_dim(tile_rows, source, 0, keepdims=False)
    col_ids = lax.dynamic_index_in_dim(tile_cols, source, 0, keepdims=False)
    number = lax.dynamic_index_in_dim(tile_counts, source, 0, keepdims=False)
    live = (jnp.arange(slots) < number).astype(jnp.float32)
    return (values, row_ids, col_ids, live)


def add_forward(totals, piece, parts, keep):
    values, row_ids, col_ids, live = parts
    blocks_in = piece.reshape(piece.shape[0], -1, values.shape[1])
    block_count = blocks_in.shape[1]
    pick = jax.nn.one_hot(col_ids, block_count, dtype=jnp.bfloat16)
    chosen = jnp.einsum("frm,sr->fsm", blocks_in, pick, preferred_element_type=jnp.float32).astype(
        jnp.bfloat16
    )
    product = jnp.einsum("fsm,sjm->fsj", chosen, values, preferred_element_type=jnp.float32)
    place = jax.nn.one_hot(row_ids, block_count, dtype=jnp.float32) * (live * keep)[:, None]
    return totals + jnp.einsum("fsj,sr->frj", product, place)


def add_backward(totals, grad_blocks, parts, keep):
    values, row_ids, col_ids, live = parts
    block_count = grad_blocks.shape[1]
    pick = jax.nn.one_hot(row_ids, block_count, dtype=jnp.bfloat16)
    chosen = jnp.einsum(
        "frj,sr->fsj", grad_blocks, pick, preferred_element_type=jnp.float32
    ).astype(jnp.bfloat16)
    product = jnp.einsum("fsj,sjm->fsm", chosen, values, preferred_element_type=jnp.float32)
    place = jax.nn.one_hot(col_ids, block_count, dtype=jnp.float32) * (live * keep)[:, None]
    return totals + jnp.einsum("fsm,sc->fcm", product, place)


def per_device(features, tile_values, tile_rows, tile_cols, tile_counts, weight, cotangent):
    node_count = lax.axis_size("node")
    own_index = lax.axis_index("node")
    slice_width = features.shape[0]
    local_nodes = features.shape[1]
    tile_side = tile_values.shape[1]
    block_count = local_nodes // tile_side

    def pair_of(source):
        return select_pair(tile_values, tile_rows, tile_cols, tile_counts, source)

    totals = jnp.zeros((slice_width, block_count, tile_side), jnp.float32)
    totals = add_forward(totals, features, pair_of(own_index), 1.0)

    def ahead_step(step, carry):
        running, moving = carry
        moving = passed_along(moving, "node", 1)
        source = (own_index - step) % node_count
        return (add_forward(running, moving, pair_of(source), 1.0), moving)

    totals, _ = lax.fori_loop(1, node_count, ahead_step, (totals, features))
    aggregated = totals.reshape(slice_width, local_nodes).astype(jnp.bfloat16)
    full_rows = lax.all_to_all(aggregated, "feat", split_axis=1, concat_axis=0, tiled=True)
    pre = jnp.dot(weight.T, full_rows, preferred_element_type=jnp.float32)
    activated = jax.nn.silu(pre).astype(jnp.bfloat16)
    sigma = jax.nn.sigmoid(pre)
    dpre = (cotangent.astype(jnp.float32) * sigma * (1.0 + pre * (1.0 - sigma))).astype(
        jnp.bfloat16
    )
    weight_part = lax.dot_general(
        full_rows, dpre, (((1,), (1,)), ((), ())), preferred_element_type=jnp.float32
    )
    grad_weight = lax.psum(weight_part, ("node", "feat"))
    dagg = jnp.dot(weight, dpre, preferred_element_type=jnp.float32).astype(jnp.bfloat16)
    grad_slices = lax.all_to_all(dagg, "feat", split_axis=0, concat_axis=1, tiled=True)
    grad_blocks = grad_slices.reshape(slice_width, block_count, tile_side)
    zeros = jnp.zeros((slice_width, block_count, tile_side), jnp.float32)
    start = add_backward(zeros, grad_blocks, pair_of((own_index - 1) % node_count), 1.0)

    def carry_step(step, running):
        running = passed_along(running, "node", 1)
        owner = (own_index - step - 1) % node_count
        return add_backward(running, grad_blocks, pair_of(owner), 1.0)

    gradient = lax.fori_loop(1, node_count, carry_step, start)
    return (activated, grad_weight, gradient.reshape(slice_width, local_nodes))


def solution(mesh):
    placed = (
        P("feat", "node"),
        P("node", None, None),
        P("node", None),
        P("node", None),
        P("node"),
        P(),
        P(None, ("node", "feat")),
    )
    return jax.shard_map(
        per_device,
        mesh=mesh,
        in_specs=placed,
        out_specs=(P(None, ("node", "feat")), P(), P("feat", "node")),
        check_vma=False,
    )
```

profile of v0, /device:TPU:0, one launch (start us, length us, event | category | flops | bytes accessed | tf_op | source)
XLA Modules:
  0.0 227.0 jit_solution(9543807741233657913)
XLA Ops:
  7.2 0.9 copy.98
  8.1 0.7 copy-done.2
  11.7 1.1 fusion.47
  12.9 62.7 %while.32 = (s32[]{:T(128)}, f32[64,4,128]{2,1,0:T(4,128)S(1)}, bf16[64,512]{1,0:T(8,128)(2,1)S(1)}, s32[]{:T(128)}, s32[8,4]{1,0:T(8,128)S(1)}, /*index=5*/s32[...) while((s32[]{:T(128)}, f32[64,4,128]{2,1,0:T(4,128)S(1)}, ...), condition=%wide.region_1.2_spmd, body=%wide.region_0.1_spmd.sunk | while | flops 8945741 | bytes 1245694 | solution.py:67
  12.9 3.0 %collective-permute-start = (bf16[64,512]{1,0:T(8,128)(2,1)S(1)}, bf16[64,512]{1,0:T(8,128)(2,1)S(1)}, u32[]{:S(2)}, u32[]{:S(2)}) collective-permute-start(bf16[64,512]{1,0:T(8,128)(2,1)S(1)} %get-tuple-element.610), channel_id=1, source_target_pairs={{0,4},{4,8},{8,12},{12,16},{16,20},{20,24},{24,28},{28,0},{1,5},{5... | collective-permute-start | bytes 196616 | tf_op jit(solution)/shard_map/while/body/eval_jaxpr/ppermute | solution.py:9
  17.2 4.0 %collective-permute-done = bf16[64,512]{1,0:T(8,128)(2,1)S(1)} collective-permute-done((bf16[64,512]{1,0:T(8,128)(2,1)S(1)}, bf16[64,512]{1,0:T(8,128)(2,1)S(1)}, u32[]{:S(2)}, u32[]{:S(2)}) %collective-permute-start) | collective-permute-done | bytes 65568 | tf_op jit(solution)/shard_map/while/body/eval_jaxpr/ppermute | solution.py:9
  21.5 1.1 fusion.115
  24.3 5.7 %collective-permute-done = bf16[64,512]{1,0:T(8,128)(2,1)S(1)} collective-permute-done((bf16[64,512]{1,0:T(8,128)(2,1)S(1)}, bf16[64,512]{1,0:T(8,128)(2,1)S(1)}, u32[]{:S(2)}, u32[]{:S(2)}) %collective-permute-start) | collective-permute-done | bytes 65568 | tf_op jit(solution)/shard_map/while/body/eval_jaxpr/ppermute | solution.py:9
  30.3 1.1 fusion.115
  33.1 5.7 %collective-permute-done = bf16[64,512]{1,0:T(8,128)(2,1)S(1)} collective-permute-done((bf16[64,512]{1,0:T(8,128)(2,1)S(1)}, bf16[64,512]{1,0:T(8,128)(2,1)S(1)}, u32[]{:S(2)}, u32[]{:S(2)}) %collective-permute-start) | collective-permute-done | bytes 65568 | tf_op jit(solution)/shard_map/while/body/eval_jaxpr/ppermute | solution.py:9
  39.0 1.1 fusion.115
  41.9 5.7 %collective-permute-done = bf16[64,512]{1,0:T(8,128)(2,1)S(1)} collective-permute-done((bf16[64,512]{1,0:T(8,128)(2,1)S(1)}, bf16[64,512]{1,0:T(8,128)(2,1)S(1)}, u32[]{:S(2)}, u32[]{:S(2)}) %collective-permute-start) | collective-permute-done | bytes 65568 | tf_op jit(solution)/shard_map/while/body/eval_jaxpr/ppermute | solution.py:9
  47.8 1.1 fusion.115
  50.6 5.7 %collective-permute-done = bf16[64,512]{1,0:T(8,128)(2,1)S(1)} collective-permute-done((bf16[64,512]{1,0:T(8,128)(2,1)S(1)}, bf16[64,512]{1,0:T(8,128)(2,1)S(1)}, u32[]{:S(2)}, u32[]{:S(2)}) %collective-permute-start) | collective-permute-done | bytes 65568 | tf_op jit(solution)/shard_map/while/body/eval_jaxpr/ppermute | solution.py:9
  56.6 1.1 fusion.115
  59.4 5.7 %collective-permute-done = bf16[64,512]{1,0:T(8,128)(2,1)S(1)} collective-permute-done((bf16[64,512]{1,0:T(8,128)(2,1)S(1)}, bf16[64,512]{1,0:T(8,128)(2,1)S(1)}, u32[]{:S(2)}, u32[]{:S(2)}) %collective-permute-start) | collective-permute-done | bytes 65568 | tf_op jit(solution)/shard_map/while/body/eval_jaxpr/ppermute | solution.py:9
  65.3 1.1 fusion.115
  68.2 5.7 %collective-permute-done = bf16[64,512]{1,0:T(8,128)(2,1)S(1)} collective-permute-done((bf16[64,512]{1,0:T(8,128)(2,1)S(1)}, bf16[64,512]{1,0:T(8,128)(2,1)S(1)}, u32[]{:S(2)}, u32[]{:S(2)}) %collective-permute-start) | collective-permute-done | bytes 65568 | tf_op jit(solution)/shard_map/while/body/eval_jaxpr/ppermute | solution.py:9
  74.1 1.1 fusion.115
  76.2 3.4 %all-to-all-start = ((bf16[64,4,128]{2,0,1:T(8,128)(2,1)}), bf16[64,4,128]{2,0,1:T(8,128)(2,1)S(1)}, u32[]{:S(2)}, u32[]{:S(2)}) async-start(bf16[64,4,128]{2,0,1:T(8,128)(2,1)} %copy.71), calls=%async_computation | async-start | bytes 131072 | tf_op jit(solution)/shard_map/all_to_all | solution.py:69
  79.7 0.7 compare_convert_fusion.2
  80.5 3.3 %all-to-all-done = bf16[64,4,128]{2,0,1:T(8,128)(2,1)S(1)} async-done(((bf16[64,4,128]{2,0,1:T(8,128)(2,1)}), bf16[64,4,128]{2,0,1:T(8,128)(2,1)S(1)}, u32[]{:S(2)}, u32[]{:S(2)}) %all-to-all-start) | async-done | bytes 65568 | tf_op jit(solution)/shard_map/all_to_all | solution.py:69
  84.2 0.7 copy.21
  84.9 3.3 %all-to-all-start.1 = ((bf16[4,64,128]{2,1,0:T(8,128)(2,1)}), bf16[4,64,128]{2,1,0:T(8,128)(2,1)S(1)}, u32[]{:S(2)}, u32[]{:S(2)}) async-start(bf16[4,64,128]{2,1,0:T(8,128)(2,1)} %bitcast.30), calls=%async_computation.1 | async-start | bytes 131072 | tf_op jit(solution)/shard_map/all_to_all | solution.py:81
  88.3 0.9 fusion.77
  89.2 0.7 copy.25
  89.9 2.4 %all-to-all-done.1 = bf16[4,64,128]{2,1,0:T(8,128)(2,1)S(1)} async-done(((bf16[4,64,128]{2,1,0:T(8,128)(2,1)}), bf16[4,64,128]{2,1,0:T(8,128)(2,1)S(1)}, u32[]{:S(2)}, u32[]{:S(2)}) %all-to-all-start.1) | async-done | bytes 65568 | tf_op jit(solution)/shard_map/all_to_all | solution.py:81
  92.6 1.1 fusion.45
  93.9 58.6 %while.33 = (s32[]{:T(128)}, f32[64,4,128]{2,1,0:T(4,128)S(1)}, s32[]{:T(128)}, s32[8,4]{1,0:T(8,128)S(1)}, s32[8]{0:T(128)S(1)}, /*index=5*/bf16[32,128,128]{2,...) while((s32[]{:T(128)}, f32[64,4,128]{2,1,0:T(4,128)S(1)}, ...), condition=%wide.region_4.5_spmd, body=%wide.region_3.4_spmd.sunk | while | flops 8945742 | bytes 1245714 | solution.py:91
  94.2 1.1 fusion.125
  96.5 5.2 %collective-permute-done.1 = f32[64,4,128]{2,1,0:T(4,128)S(1)} collective-permute-done((f32[64,4,128]{2,1,0:T(4,128)S(1)}, f32[64,4,128]{2,1,0:T(4,128)S(1)}, u32[]{:S(2)}, u32[]{:S(2)}) %collective-permute-start.1) | collective-permute-done | bytes 131104 | tf_op jit(solution)/shard_map/while/body/eval_jaxpr/ppermute | solution.py:9
  102.5 1.1 fusion.125
  104.8 5.2 %collective-permute-done.1 = f32[64,4,128]{2,1,0:T(4,128)S(1)} collective-permute-done((f32[64,4,128]{2,1,0:T(4,128)S(1)}, f32[64,4,128]{2,1,0:T(4,128)S(1)}, u32[]{:S(2)}, u32[]{:S(2)}) %collective-permute-start.1) | collective-permute-done | bytes 131104 | tf_op jit(solution)/shard_map/while/body/eval_jaxpr/ppermute | solution.py:9
  110.7 1.1 fusion.125
  112.4 0.6 compare_convert_fusion.7
  113.0 5.2 %collective-permute-done.1 = f32[64,4,128]{2,1,0:T(4,128)S(1)} collective-permute-done((f32[64,4,128]{2,1,0:T(4,128)S(1)}, f32[64,4,128]{2,1,0:T(4,128)S(1)}, u32[]{:S(2)}, u32[]{:S(2)}) %collective-permute-start.1) | collective-permute-done | bytes 131104 | tf_op jit(solution)/shard_map/while/body/eval_jaxpr/ppermute | solution.py:9
  118.9 1.1 fusion.125
  120.6 0.6 compare_convert_fusion.7
  121.2 5.1 %collective-permute-done.1 = f32[64,4,128]{2,1,0:T(4,128)S(1)} collective-permute-done((f32[64,4,128]{2,1,0:T(4,128)S(1)}, f32[64,4,128]{2,1,0:T(4,128)S(1)}, u32[]{:S(2)}, u32[]{:S(2)}) %collective-permute-start.1) | collective-permute-done | bytes 131104 | tf_op jit(solution)/shard_map/while/body/eval_jaxpr/ppermute | solution.py:9
  127.0 1.1 fusion.125
  129.3 5.3 %collective-permute-done.1 = f32[64,4,128]{2,1,0:T(4,128)S(1)} collective-permute-done((f32[64,4,128]{2,1,0:T(4,128)S(1)}, f32[64,4,128]{2,1,0:T(4,128)S(1)}, u32[]{:S(2)}, u32[]{:S(2)}) %collective-permute-start.1) | collective-permute-done | bytes 131104 | tf_op jit(solution)/shard_map/while/body/eval_jaxpr/ppermute | solution.py:9
  135.4 1.1 fusion.125
  137.7 6.3 %collective-permute-done.1 = f32[64,4,128]{2,1,0:T(4,128)S(1)} collective-permute-done((f32[64,4,128]{2,1,0:T(4,128)S(1)}, f32[64,4,128]{2,1,0:T(4,128)S(1)}, u32[]{:S(2)}, u32[]{:S(2)}) %collective-permute-start.1) | collective-permute-done | bytes 131104 | tf_op jit(solution)/shard_map/while/body/eval_jaxpr/ppermute | solution.py:9
  144.7 1.1 fusion.125
  147.0 5.2 %collective-permute-done.1 = f32[64,4,128]{2,1,0:T(4,128)S(1)} collective-permute-done((f32[64,4,128]{2,1,0:T(4,128)S(1)}, f32[64,4,128]{2,1,0:T(4,128)S(1)}, u32[]{:S(2)}, u32[]{:S(2)}) %collective-permute-start.1) | collective-permute-done | bytes 131104 | tf_op jit(solution)/shard_map/while/body/eval_jaxpr/ppermute | solution.py:9
  152.5 0.7 copy.72
  153.2 65.3 %all-reduce.2.cloned.1.call-done = f32[256,256]{1,0:T(8,128)} async-done(((f32[256,256]{1,0:T(8,128)}), f32[256,256]{1,0:T(8,128)}) %all-reduce.2.cloned.1.call-update) | async-done | bytes 262160 | tf_op jit(solution)/shard_map/psum | solution.py:79
  218.5 1.7 copy.99
  (121 shorter events, 30.4 us)
Async XLA Ops:
  7.2 76.6 %copy-start = (bf16[256,256]{1,0:T(8,128)(2,1)S(1)}, bf16[256,256]{1,0:T(8,128)(2,1)}, u32[]{:S(2)}) copy-start(bf16[256,256]{1,0:T(8,128)(2,1)} %param.16) | copy-start | bytes 393220
  8.1 0.7 copy-start.2
  8.7 0.7 copy-start.3
  9.5 0.7 copy-start.4
  12.9 8.3 %collective-permute-start = (bf16[64,512]{1,0:T(8,128)(2,1)S(1)}, bf16[64,512]{1,0:T(8,128)(2,1)S(1)}, u32[]{:S(2)}, u32[]{:S(2)}) collective-permute-start(bf16[64,512]{1,0:T(8,128)(2,1)S(1)} %get-tuple-element.610), channel_id=1, source_target_pairs={{0,4},{4,8},{8,12},{12,16},{16,20},{20,24},{24,28},{28,0},{1,5},{5... | collective-permute-start | bytes 196616 | tf_op jit(solution)/shard_map/while/body/eval_jaxpr/ppermute | solution.py:9
  23.0 7.0 %collective-permute-start = (bf16[64,512]{1,0:T(8,128)(2,1)S(1)}, bf16[64,512]{1,0:T(8,128)(2,1)S(1)}, u32[]{:S(2)}, u32[]{:S(2)}) collective-permute-start(bf16[64,512]{1,0:T(8,128)(2,1)S(1)} %get-tuple-element.610), channel_id=1, source_target_pairs={{0,4},{4,8},{8,12},{12,16},{16,20},{20,24},{24,28},{28,0},{1,5},{5... | collective-permute-start | bytes 196616 | tf_op jit(solution)/shard_map/while/body/eval_jaxpr/ppermute | solution.py:9
  31.7 7.0 %collective-permute-start = (bf16[64,512]{1,0:T(8,128)(2,1)S(1)}, bf16[64,512]{1,0:T(8,128)(2,1)S(1)}, u32[]{:S(2)}, u32[]{:S(2)}) collective-permute-start(bf16[64,512]{1,0:T(8,128)(2,1)S(1)} %get-tuple-element.610), channel_id=1, source_target_pairs={{0,4},{4,8},{8,12},{12,16},{16,20},{20,24},{24,28},{28,0},{1,5},{5... | collective-permute-start | bytes 196616 | tf_op jit(solution)/shard_map/while/body/eval_jaxpr/ppermute | solution.py:9
  40.5 7.0 %collective-permute-start = (bf16[64,512]{1,0:T(8,128)(2,1)S(1)}, bf16[64,512]{1,0:T(8,128)(2,1)S(1)}, u32[]{:S(2)}, u32[]{:S(2)}) collective-permute-start(bf16[64,512]{1,0:T(8,128)(2,1)S(1)} %get-tuple-element.610), channel_id=1, source_target_pairs={{0,4},{4,8},{8,12},{12,16},{16,20},{20,24},{24,28},{28,0},{1,5},{5... | collective-permute-start | bytes 196616 | tf_op jit(solution)/shard_map/while/body/eval_jaxpr/ppermute | solution.py:9
  49.3 7.0 %collective-permute-start = (bf16[64,512]{1,0:T(8,128)(2,1)S(1)}, bf16[64,512]{1,0:T(8,128)(2,1)S(1)}, u32[]{:S(2)}, u32[]{:S(2)}) collective-permute-start(bf16[64,512]{1,0:T(8,128)(2,1)S(1)} %get-tuple-element.610), channel_id=1, source_target_pairs={{0,4},{4,8},{8,12},{12,16},{16,20},{20,24},{24,28},{28,0},{1,5},{5... | collective-permute-start | bytes 196616 | tf_op jit(solution)/shard_map/while/body/eval_jaxpr/ppermute | solution.py:9
  58.1 7.0 %collective-permute-start = (bf16[64,512]{1,0:T(8,128)(2,1)S(1)}, bf16[64,512]{1,0:T(8,128)(2,1)S(1)}, u32[]{:S(2)}, u32[]{:S(2)}) collective-permute-start(bf16[64,512]{1,0:T(8,128)(2,1)S(1)} %get-tuple-element.610), channel_id=1, source_target_pairs={{0,4},{4,8},{8,12},{12,16},{16,20},{20,24},{24,28},{28,0},{1,5},{5... | collective-permute-start | bytes 196616 | tf_op jit(solution)/shard_map/while/body/eval_jaxpr/ppermute | solution.py:9
  66.8 7.0 %collective-permute-start = (bf16[64,512]{1,0:T(8,128)(2,1)S(1)}, bf16[64,512]{1,0:T(8,128)(2,1)S(1)}, u32[]{:S(2)}, u32[]{:S(2)}) collective-permute-start(bf16[64,512]{1,0:T(8,128)(2,1)S(1)} %get-tuple-element.610), channel_id=1, source_target_pairs={{0,4},{4,8},{8,12},{12,16},{16,20},{20,24},{24,28},{28,0},{1,5},{5... | collective-permute-start | bytes 196616 | tf_op jit(solution)/shard_map/while/body/eval_jaxpr/ppermute | solution.py:9
  76.2 4.1 %copy-start.1 = (bf16[256,128]{1,0:T(8,128)(2,1)S(1)}, bf16[256,128]{1,0:T(8,128)(2,1)}, u32[]{:S(2)}) copy-start(bf16[256,128]{1,0:T(8,128)(2,1)} %param.17) | copy-start | bytes 196612
  76.2 7.5 %all-to-all-start = ((bf16[64,4,128]{2,0,1:T(8,128)(2,1)}), bf16[64,4,128]{2,0,1:T(8,128)(2,1)S(1)}, u32[]{:S(2)}, u32[]{:S(2)}) async-start(bf16[64,4,128]{2,0,1:T(8,128)(2,1)} %copy.71), calls=%async_computation | async-start | bytes 131072 | tf_op jit(solution)/shard_map/all_to_all | solution.py:69
  84.9 7.4 %all-to-all-start.1 = ((bf16[4,64,128]{2,1,0:T(8,128)(2,1)}), bf16[4,64,128]{2,1,0:T(8,128)(2,1)S(1)}, u32[]{:S(2)}, u32[]{:S(2)}) async-start(bf16[4,64,128]{2,1,0:T(8,128)(2,1)} %bitcast.30), calls=%async_computation.1 | async-start | bytes 131072 | tf_op jit(solution)/shard_map/all_to_all | solution.py:81
  88.2 130.3 %all-reduce.2.cloned.1.call-start = ((), (), s32[]{:S(2)}) async-start(), calls=%async_computation.2 | async-start | bytes 524288 | tf_op jit(solution)/shard_map/psum | solution.py:79
  93.9 7.9 %collective-permute-start.1 = (f32[64,4,128]{2,1,0:T(4,128)S(1)}, f32[64,4,128]{2,1,0:T(4,128)S(1)}, u32[]{:S(2)}, u32[]{:S(2)}) collective-permute-start(f32[64,4,128]{2,1,0:T(4,128)S(1)} %get-tuple-element.652), channel_id=1, source_target_pairs={{0,4},{4,8},{8,12},{12,16},{16,20},{20,24},{24,28},{28,0},{1,5},{5... | collective-permute-start | bytes 393224 | tf_op jit(solution)/shard_map/while/body/eval_jaxpr/ppermute | solution.py:9
  102.1 7.9 %collective-permute-start.1 = (f32[64,4,128]{2,1,0:T(4,128)S(1)}, f32[64,4,128]{2,1,0:T(4,128)S(1)}, u32[]{:S(2)}, u32[]{:S(2)}) collective-permute-start(f32[64,4,128]{2,1,0:T(4,128)S(1)} %get-tuple-element.652), channel_id=1, source_target_pairs={{0,4},{4,8},{8,12},{12,16},{16,20},{20,24},{24,28},{28,0},{1,5},{5... | collective-permute-start | bytes 393224 | tf_op jit(solution)/shard_map/while/body/eval_jaxpr/ppermute | solution.py:9
  110.4 7.9 %collective-permute-start.1 = (f32[64,4,128]{2,1,0:T(4,128)S(1)}, f32[64,4,128]{2,1,0:T(4,128)S(1)}, u32[]{:S(2)}, u32[]{:S(2)}) collective-permute-start(f32[64,4,128]{2,1,0:T(4,128)S(1)} %get-tuple-element.652), channel_id=1, source_target_pairs={{0,4},{4,8},{8,12},{12,16},{16,20},{20,24},{24,28},{28,0},{1,5},{5... | collective-permute-start | bytes 393224 | tf_op jit(solution)/shard_map/while/body/eval_jaxpr/ppermute | solution.py:9
  118.6 7.7 %collective-permute-start.1 = (f32[64,4,128]{2,1,0:T(4,128)S(1)}, f32[64,4,128]{2,1,0:T(4,128)S(1)}, u32[]{:S(2)}, u32[]{:S(2)}) collective-permute-start(f32[64,4,128]{2,1,0:T(4,128)S(1)} %get-tuple-element.652), channel_id=1, source_target_pairs={{0,4},{4,8},{8,12},{12,16},{16,20},{20,24},{24,28},{28,0},{1,5},{5... | collective-permute-start | bytes 393224 | tf_op jit(solution)/shard_map/while/body/eval_jaxpr/ppermute | solution.py:9
  126.7 8.0 %collective-permute-start.1 = (f32[64,4,128]{2,1,0:T(4,128)S(1)}, f32[64,4,128]{2,1,0:T(4,128)S(1)}, u32[]{:S(2)}, u32[]{:S(2)}) collective-permute-start(f32[64,4,128]{2,1,0:T(4,128)S(1)} %get-tuple-element.652), channel_id=1, source_target_pairs={{0,4},{4,8},{8,12},{12,16},{16,20},{20,24},{24,28},{28,0},{1,5},{5... | collective-permute-start | bytes 393224 | tf_op jit(solution)/shard_map/while/body/eval_jaxpr/ppermute | solution.py:9
  135.0 8.9 %collective-permute-start.1 = (f32[64,4,128]{2,1,0:T(4,128)S(1)}, f32[64,4,128]{2,1,0:T(4,128)S(1)}, u32[]{:S(2)}, u32[]{:S(2)}) collective-permute-start(f32[64,4,128]{2,1,0:T(4,128)S(1)} %get-tuple-element.652), channel_id=1, source_target_pairs={{0,4},{4,8},{8,12},{12,16},{16,20},{20,24},{24,28},{28,0},{1,5},{5... | collective-permute-start | bytes 393224 | tf_op jit(solution)/shard_map/while/body/eval_jaxpr/ppermute | solution.py:9
  144.3 7.8 %collective-permute-start.1 = (f32[64,4,128]{2,1,0:T(4,128)S(1)}, f32[64,4,128]{2,1,0:T(4,128)S(1)}, u32[]{:S(2)}, u32[]{:S(2)}) collective-permute-start(f32[64,4,128]{2,1,0:T(4,128)S(1)} %get-tuple-element.652), channel_id=1, source_target_pairs={{0,4},{4,8},{8,12},{12,16},{16,20},{20,24},{24,28},{28,0},{1,5},{5... | collective-permute-start | bytes 393224 | tf_op jit(solution)/shard_map/while/body/eval_jaxpr/ppermute | solution.py:9
Sparse Core Ops, SparseCore 0:
  95.1 123.3 all-reduce.1
where the time goes:
time: 228 us; the launch traced here: 227 us
  waiting for transfers between devices  147 us (64%)
  matrix products  27.7 us (12%)
  local copies, waits for them, and re-layouts  16.8 us (7%)
  between operations  14.2 us (6%)
  starting transfers between devices  10.5 us (5%)
  other arithmetic  10.4 us (5%)
    ppermute x14, waiting for transfers between devices, passed_along(): return lax.ppermute(x, axis, [(i, (i + by) % count) for i in range(count)])  75.5 us
    psum x1, waiting for transfers between devices, per_device(): grad_weight = lax.psum(weight_part, ('node', 'feat'))  65.3 us
    convert_element_type x16, other arithmetic, select_pair(): live = (jnp.arange(slots) < number).astype(jnp.float32)  10.4 us
    dynamic_slice x15, local copies, waits for them, and re-layouts, select_pair(): number = lax.dynamic_index_in_dim(tile_counts, source, 0, keepdims=False)  8.87 us
    dot_general x8, matrix products, add_forward(): jnp.einsum('fsm,sjm->fsj', chosen, values, preferred_element_type=jnp.flo...  8.64 us
    dot_general x8, matrix products, add_backward(): jnp.einsum('fsj,sjm->fsm', chosen, values, preferred_element_type=jnp.flo...  8.47 us
    unnamed x15, local copies, waits for them, and re-layouts  5.78 us
  transfers between devices with their start and end apart: 17, of which 17 were waited for; matrix products, arithmetic and copies ran while one was open for 15% of the time, Pallas kernels for 0%

commit v1 on v0

--- a/solution.py
+++ b/solution.py
@@ -76,7 +76,8 @@
     weight_part = lax.dot_general(
         full_rows, dpre, (((1,), (1,)), ((), ())), preferred_element_type=jnp.float32
     )
-    grad_weight = lax.psum(weight_part, ("node", "feat"))
+    shards = lax.all_gather(weight_part, ("node", "feat"), axis=0, tiled=False)
+    grad_weight = shards.sum(axis=0)
     dagg = jnp.dot(weight, dpre, preferred_element_type=jnp.float32).astype(jnp.bfloat16)
     grad_slices = lax.all_to_all(dagg, "feat", split_axis=0, concat_axis=1, tiled=True)
     grad_blocks = grad_slices.reshape(slice_width, block_count, tile_side)

time: 228 us -> 184 us (0.81)
  waiting for transfers between devices: 147 us -> 87.3 us
  local copies, waits for them, and re-layouts: 16.8 us -> 26.2 us
  other arithmetic: 10.4 us -> 14.9 us
    psum x1 -> x0, waiting for transfers between devices: 65.3 us -> none  [per_device(): grad_weight = lax.psum(weight_part, ('node', 'feat'))]
    dynamic_slice x15, local copies, waits for them, and re-layouts: 8.87 us -> 18.8 us  [select_pair(): number = lax.dynamic_index_in_dim(tile_counts, source, 0, keepdims=False)]
    reduce_sum x0 -> x1, other arithmetic: none -> 4.63 us  [per_device(): grad_weight = shards.sum(axis=0)]
    ppermute x14, waiting for transfers between devices: 75.5 us -> 79.9 us  [passed_along(): return lax.ppermute(x, axis, [(i, (i + by) % count) for i in range(count)])]
    unnamed x15 -> x6, local copies, waits for them, and re-layouts: 5.78 us -> 3.23 us
  transfers between devices with their start and end apart: 17 -> 17, of which waited for: 17 -> 17; matrix products, arithmetic and copies ran while one was open for 15% -> 24% of each run, Pallas kernels for 0% -> 0%
where the time goes in v1:
time: 184 us; the launch traced here: 182 us
  waiting for transfers between devices  87.3 us (47%)
  matrix products  27.7 us (15%)
  local copies, waits for them, and re-layouts  26.2 us (14%)
  other arithmetic  14.9 us (8%)
  between operations  14.2 us (8%)
  starting transfers between devices  10.4 us (6%)
    ppermute x14, waiting for transfers between devices, passed_along(): return lax.ppermute(x, axis, [(i, (i + by) % count) for i in range(count)])  79.9 us
    dynamic_slice x15, local copies, waits for them, and re-layouts, select_pair(): number = lax.dynamic_index_in_dim(tile_counts, source, 0, keepdims=False)  18.8 us
    convert_element_type x16, other arithmetic, select_pair(): live = (jnp.arange(slots) < number).astype(jnp.float32)  10.3 us
    dot_general x8, matrix products, add_forward(): jnp.einsum('fsm,sjm->fsj', chosen, values, preferred_element_type=jnp.flo...  8.63 us
    dot_general x8, matrix products, add_backward(): jnp.einsum('fsj,sjm->fsm', chosen, values, preferred_element_type=jnp.flo...  8.5 us
    reduce_sum x1, other arithmetic, per_device(): grad_weight = shards.sum(axis=0)  4.63 us
    ppermute x14, starting transfers between devices, passed_along(): return lax.ppermute(x, axis, [(i, (i + by) % count) for i in range(count)])  3.75 us
  transfers between devices with their start and end apart: 17, of which 17 were waited for; matrix products, arithmetic and copies ran while one was open for 24% of the time, Pallas kernels for 0%

profile of v1, /device:TPU:0, one launch (start us, length us, event | category | flops | bytes accessed | tf_op | source)
XLA Modules:
  0.0 181.6 jit_solution(3731943378391240382)
XLA Ops:
  10.6 1.3 fusion.76
  12.8 1.1 fusion.47
  14.1 62.6 %while.32 = (s32[]{:T(128)}, f32[64,4,128]{2,1,0:T(4,128)S(1)}, bf16[64,512]{1,0:T(8,128)(2,1)S(1)}, s32[]{:T(128)}, s32[8,4]{1,0:T(8,128)S(1)}, /*index=5*/s32[...) while((s32[]{:T(128)}, f32[64,4,128]{2,1,0:T(4,128)S(1)}, ...), condition=%wide.region_1.2_spmd, body=%wide.region_0.1_spmd.sunk | while | flops 8945741 | bytes 1245694 | solution.py:67
  14.1 3.0 %collective-permute-start = (bf16[64,512]{1,0:T(8,128)(2,1)S(1)}, bf16[64,512]{1,0:T(8,128)(2,1)S(1)}, u32[]{:S(2)}, u32[]{:S(2)}) collective-permute-start(bf16[64,512]{1,0:T(8,128)(2,1)S(1)} %get-tuple-element.610), channel_id=1, source_target_pairs={{0,4},{4,8},{8,12},{12,16},{16,20},{20,24},{24,28},{28,0},{1,5},{5... | collective-permute-start | bytes 196616 | tf_op jit(solution)/shard_map/while/body/eval_jaxpr/ppermute | solution.py:9
  17.1 1.2 dynamic_slice.148
  19.0 3.4 %collective-permute-done = bf16[64,512]{1,0:T(8,128)(2,1)S(1)} collective-permute-done((bf16[64,512]{1,0:T(8,128)(2,1)S(1)}, bf16[64,512]{1,0:T(8,128)(2,1)S(1)}, u32[]{:S(2)}, u32[]{:S(2)}) %collective-permute-start) | collective-permute-done | bytes 65568 | tf_op jit(solution)/shard_map/while/body/eval_jaxpr/ppermute | solution.py:9
  22.6 1.1 fusion.115
  24.2 1.2 dynamic_slice.148
  26.1 5.0 %collective-permute-done = bf16[64,512]{1,0:T(8,128)(2,1)S(1)} collective-permute-done((bf16[64,512]{1,0:T(8,128)(2,1)S(1)}, bf16[64,512]{1,0:T(8,128)(2,1)S(1)}, u32[]{:S(2)}, u32[]{:S(2)}) %collective-permute-start) | collective-permute-done | bytes 65568 | tf_op jit(solution)/shard_map/while/body/eval_jaxpr/ppermute | solution.py:9
  31.4 1.1 fusion.115
  33.0 1.2 dynamic_slice.148
  34.9 5.0 %collective-permute-done = bf16[64,512]{1,0:T(8,128)(2,1)S(1)} collective-permute-done((bf16[64,512]{1,0:T(8,128)(2,1)S(1)}, bf16[64,512]{1,0:T(8,128)(2,1)S(1)}, u32[]{:S(2)}, u32[]{:S(2)}) %collective-permute-start) | collective-permute-done | bytes 65568 | tf_op jit(solution)/shard_map/while/body/eval_jaxpr/ppermute | solution.py:9
  40.1 1.1 fusion.115
  41.7 1.2 dynamic_slice.148
  43.6 5.0 %collective-permute-done = bf16[64,512]{1,0:T(8,128)(2,1)S(1)} collective-permute-done((bf16[64,512]{1,0:T(8,128)(2,1)S(1)}, bf16[64,512]{1,0:T(8,128)(2,1)S(1)}, u32[]{:S(2)}, u32[]{:S(2)}) %collective-permute-start) | collective-permute-done | bytes 65568 | tf_op jit(solution)/shard_map/while/body/eval_jaxpr/ppermute | solution.py:9
  48.9 1.1 fusion.115
  50.5 1.2 dynamic_slice.148
  52.4 5.0 %collective-permute-done = bf16[64,512]{1,0:T(8,128)(2,1)S(1)} collective-permute-done((bf16[64,512]{1,0:T(8,128)(2,1)S(1)}, bf16[64,512]{1,0:T(8,128)(2,1)S(1)}, u32[]{:S(2)}, u32[]{:S(2)}) %collective-permute-start) | collective-permute-done | bytes 65568 | tf_op jit(solution)/shard_map/while/body/eval_jaxpr/ppermute | solution.py:9
  57.7 1.1 fusion.115
  59.3 1.2 dynamic_slice.148
  61.2 5.0 %collective-permute-done = bf16[64,512]{1,0:T(8,128)(2,1)S(1)} collective-permute-done((bf16[64,512]{1,0:T(8,128)(2,1)S(1)}, bf16[64,512]{1,0:T(8,128)(2,1)S(1)}, u32[]{:S(2)}, u32[]{:S(2)}) %collective-permute-start) | collective-permute-done | bytes 65568 | tf_op jit(solution)/shard_map/while/body/eval_jaxpr/ppermute | solution.py:9
  66.5 1.1 fusion.115
  68.0 1.2 dynamic_slice.148
  70.0 5.0 %collective-permute-done = bf16[64,512]{1,0:T(8,128)(2,1)S(1)} collective-permute-done((bf16[64,512]{1,0:T(8,128)(2,1)S(1)}, bf16[64,512]{1,0:T(8,128)(2,1)S(1)}, u32[]{:S(2)}, u32[]{:S(2)}) %collective-permute-start) | collective-permute-done | bytes 65568 | tf_op jit(solution)/shard_map/while/body/eval_jaxpr/ppermute | solution.py:9
  75.2 1.1 fusion.115
  77.4 3.3 %all-to-all-start = ((bf16[64,4,128]{2,0,1:T(8,128)(2,1)}), bf16[64,4,128]{2,0,1:T(8,128)(2,1)S(1)}, u32[]{:S(2)}, u32[]{:S(2)}) async-start(bf16[64,4,128]{2,0,1:T(8,128)(2,1)} %copy.71), calls=%async_computation | async-start | bytes 131072 | tf_op jit(solution)/shard_map/all_to_all | solution.py:69
  81.7 3.1 %all-to-all-done = bf16[64,4,128]{2,0,1:T(8,128)(2,1)S(1)} async-done(((bf16[64,4,128]{2,0,1:T(8,128)(2,1)}), bf16[64,4,128]{2,0,1:T(8,128)(2,1)S(1)}, u32[]{:S(2)}, u32[]{:S(2)}) %all-to-all-start) | async-done | bytes 65568 | tf_op jit(solution)/shard_map/all_to_all | solution.py:69
  86.8 3.3 %all-to-all-start.1 = ((bf16[4,64,128]{2,1,0:T(8,128)(2,1)}), bf16[4,64,128]{2,1,0:T(8,128)(2,1)S(1)}, u32[]{:S(2)}, u32[]{:S(2)}) async-start(bf16[4,64,128]{2,1,0:T(8,128)(2,1)} %bitcast.31), calls=%async_computation.1 | async-start | bytes 131072 | tf_op jit(solution)/shard_map/all_to_all | solution.py:82
  91.4 3.0 %all-to-all-done.1 = bf16[4,64,128]{2,1,0:T(8,128)(2,1)S(1)} async-done(((bf16[4,64,128]{2,1,0:T(8,128)(2,1)}), bf16[4,64,128]{2,1,0:T(8,128)(2,1)S(1)}, u32[]{:S(2)}, u32[]{:S(2)}) %all-to-all-start.1) | async-done | bytes 65568 | tf_op jit(solution)/shard_map/all_to_all | solution.py:82
  95.9 72.2 %while.33 = (s32[]{:T(128)}, f32[64,4,128]{2,1,0:T(4,128)S(1)}, s32[]{:T(128)}, s32[8,4]{1,0:T(8,128)S(1)}, s32[8]{0:T(128)}, /*index=5*/bf16[32,128,128]{2,1,0:...) while((s32[]{:T(128)}, f32[64,4,128]{2,1,0:T(4,128)S(1)}, ...), condition=%wide.region_4.5_spmd, body=%wide.region_3.4_spmd.sunk | while | flops 8945742 | bytes 1245714 | solution.py:92
  97.4 1.3 dynamic_slice.151
  99.3 7.5 %collective-permute-done.1 = f32[64,4,128]{2,1,0:T(4,128)S(1)} collective-permute-done((f32[64,4,128]{2,1,0:T(4,128)S(1)}, f32[64,4,128]{2,1,0:T(4,128)S(1)}, u32[]{:S(2)}, u32[]{:S(2)}) %collective-permute-start.1) | collective-permute-done | bytes 131104 | tf_op jit(solution)/shard_map/while/body/eval_jaxpr/ppermute | solution.py:9
  108.6 1.3 dynamic_slice.151
  110.5 4.5 %collective-permute-done.1 = f32[64,4,128]{2,1,0:T(4,128)S(1)} collective-permute-done((f32[64,4,128]{2,1,0:T(4,128)S(1)}, f32[64,4,128]{2,1,0:T(4,128)S(1)}, u32[]{:S(2)}, u32[]{:S(2)}) %collective-permute-start.1) | collective-permute-done | bytes 131104 | tf_op jit(solution)/shard_map/while/body/eval_jaxpr/ppermute | solution.py:9
  116.8 1.3 dynamic_slice.151
  118.7 6.2 %collective-permute-done.1 = f32[64,4,128]{2,1,0:T(4,128)S(1)} collective-permute-done((f32[64,4,128]{2,1,0:T(4,128)S(1)}, f32[64,4,128]{2,1,0:T(4,128)S(1)}, u32[]{:S(2)}, u32[]{:S(2)}) %collective-permute-start.1) | collective-permute-done | bytes 131104 | tf_op jit(solution)/shard_map/while/body/eval_jaxpr/ppermute | solution.py:9
  125.6 1.1 fusion.125
  126.7 1.3 dynamic_slice.151
  128.6 6.4 %collective-permute-done.1 = f32[64,4,128]{2,1,0:T(4,128)S(1)} collective-permute-done((f32[64,4,128]{2,1,0:T(4,128)S(1)}, f32[64,4,128]{2,1,0:T(4,128)S(1)}, u32[]{:S(2)}, u32[]{:S(2)}) %collective-permute-start.1) | collective-permute-done | bytes 131104 | tf_op jit(solution)/shard_map/while/body/eval_jaxpr/ppermute | solution.py:9
  136.8 1.3 dynamic_slice.151
  138.7 7.1 %collective-permute-done.1 = f32[64,4,128]{2,1,0:T(4,128)S(1)} collective-permute-done((f32[64,4,128]{2,1,0:T(4,128)S(1)}, f32[64,4,128]{2,1,0:T(4,128)S(1)}, u32[]{:S(2)}, u32[]{:S(2)}) %collective-permute-start.1) | collective-permute-done | bytes 131104 | tf_op jit(solution)/shard_map/while/body/eval_jaxpr/ppermute | solution.py:9
  147.6 1.3 dynamic_slice.151
  149.5 7.6 %collective-permute-done.1 = f32[64,4,128]{2,1,0:T(4,128)S(1)} collective-permute-done((f32[64,4,128]{2,1,0:T(4,128)S(1)}, f32[64,4,128]{2,1,0:T(4,128)S(1)}, u32[]{:S(2)}, u32[]{:S(2)}) %collective-permute-start.1) | collective-permute-done | bytes 131104 | tf_op jit(solution)/shard_map/while/body/eval_jaxpr/ppermute | solution.py:9
  157.8 1.1 fusion.125
  158.9 1.2 dynamic_slice.151
  160.8 7.0 %collective-permute-done.1 = f32[64,4,128]{2,1,0:T(4,128)S(1)} collective-permute-done((f32[64,4,128]{2,1,0:T(4,128)S(1)}, f32[64,4,128]{2,1,0:T(4,128)S(1)}, u32[]{:S(2)}, u32[]{:S(2)}) %collective-permute-start.1) | collective-permute-done | bytes 131104 | tf_op jit(solution)/shard_map/while/body/eval_jaxpr/ppermute | solution.py:9
  168.8 1.3 all-gather.3.cloned.1.call-done
  170.2 4.6 %reduce_sum.9 = f32[256,256]{1,0:T(8,128)} reduce(f32[32,256,256]{2,1,0:T(8,128)} %bitcast.127, f32[]{:T(128)} %constant.199.clone.1), dimensions={0}, to_apply=%region_2.3 | reduce | flops 2031616 | bytes 8650756 | tf_op jit(solution)/shard_map/reduce_sum | solution.py:80
  (113 shorter events, 35.5 us)
Async XLA Ops:
  7.2 77.6 %copy-start = (bf16[256,256]{1,0:T(8,128)(2,1)S(1)}, bf16[256,256]{1,0:T(8,128)(2,1)}, u32[]{:S(2)}) copy-start(bf16[256,256]{1,0:T(8,128)(2,1)} %param.16) | copy-start | bytes 393220
  14.1 8.3 %collective-permute-start = (bf16[64,512]{1,0:T(8,128)(2,1)S(1)}, bf16[64,512]{1,0:T(8,128)(2,1)S(1)}, u32[]{:S(2)}, u32[]{:S(2)}) collective-permute-start(bf16[64,512]{1,0:T(8,128)(2,1)S(1)} %get-tuple-element.610), channel_id=1, source_target_pairs={{0,4},{4,8},{8,12},{12,16},{16,20},{20,24},{24,28},{28,0},{1,5},{5... | collective-permute-start | bytes 196616 | tf_op jit(solution)/shard_map/while/body/eval_jaxpr/ppermute | solution.py:9
  24.1 7.0 %collective-permute-start = (bf16[64,512]{1,0:T(8,128)(2,1)S(1)}, bf16[64,512]{1,0:T(8,128)(2,1)S(1)}, u32[]{:S(2)}, u32[]{:S(2)}) collective-permute-start(bf16[64,512]{1,0:T(8,128)(2,1)S(1)} %get-tuple-element.610), channel_id=1, source_target_pairs={{0,4},{4,8},{8,12},{12,16},{16,20},{20,24},{24,28},{28,0},{1,5},{5... | collective-permute-start | bytes 196616 | tf_op jit(solution)/shard_map/while/body/eval_jaxpr/ppermute | solution.py:9
  32.9 7.0 %collective-permute-start = (bf16[64,512]{1,0:T(8,128)(2,1)S(1)}, bf16[64,512]{1,0:T(8,128)(2,1)S(1)}, u32[]{:S(2)}, u32[]{:S(2)}) collective-permute-start(bf16[64,512]{1,0:T(8,128)(2,1)S(1)} %get-tuple-element.610), channel_id=1, source_target_pairs={{0,4},{4,8},{8,12},{12,16},{16,20},{20,24},{24,28},{28,0},{1,5},{5... | collective-permute-start | bytes 196616 | tf_op jit(solution)/shard_map/while/body/eval_jaxpr/ppermute | solution.py:9
  41.6 7.0 %collective-permute-start = (bf16[64,512]{1,0:T(8,128)(2,1)S(1)}, bf16[64,512]{1,0:T(8,128)(2,1)S(1)}, u32[]{:S(2)}, u32[]{:S(2)}) collective-permute-start(bf16[64,512]{1,0:T(8,128)(2,1)S(1)} %get-tuple-element.610), channel_id=1, source_target_pairs={{0,4},{4,8},{8,12},{12,16},{16,20},{20,24},{24,28},{28,0},{1,5},{5... | collective-permute-start | bytes 196616 | tf_op jit(solution)/shard_map/while/body/eval_jaxpr/ppermute | solution.py:9
  50.4 7.0 %collective-permute-start = (bf16[64,512]{1,0:T(8,128)(2,1)S(1)}, bf16[64,512]{1,0:T(8,128)(2,1)S(1)}, u32[]{:S(2)}, u32[]{:S(2)}) collective-permute-start(bf16[64,512]{1,0:T(8,128)(2,1)S(1)} %get-tuple-element.610), channel_id=1, source_target_pairs={{0,4},{4,8},{8,12},{12,16},{16,20},{20,24},{24,28},{28,0},{1,5},{5... | collective-permute-start | bytes 196616 | tf_op jit(solution)/shard_map/while/body/eval_jaxpr/ppermute | solution.py:9
  59.2 7.0 %collective-permute-start = (bf16[64,512]{1,0:T(8,128)(2,1)S(1)}, bf16[64,512]{1,0:T(8,128)(2,1)S(1)}, u32[]{:S(2)}, u32[]{:S(2)}) collective-permute-start(bf16[64,512]{1,0:T(8,128)(2,1)S(1)} %get-tuple-element.610), channel_id=1, source_target_pairs={{0,4},{4,8},{8,12},{12,16},{16,20},{20,24},{24,28},{28,0},{1,5},{5... | collective-permute-start | bytes 196616 | tf_op jit(solution)/shard_map/while/body/eval_jaxpr/ppermute | solution.py:9
  68.0 7.0 %collective-permute-start = (bf16[64,512]{1,0:T(8,128)(2,1)S(1)}, bf16[64,512]{1,0:T(8,128)(2,1)S(1)}, u32[]{:S(2)}, u32[]{:S(2)}) collective-permute-start(bf16[64,512]{1,0:T(8,128)(2,1)S(1)} %get-tuple-element.610), channel_id=1, source_target_pairs={{0,4},{4,8},{8,12},{12,16},{16,20},{20,24},{24,28},{28,0},{1,5},{5... | collective-permute-start | bytes 196616 | tf_op jit(solution)/shard_map/while/body/eval_jaxpr/ppermute | solution.py:9
  77.4 7.4 %all-to-all-start = ((bf16[64,4,128]{2,0,1:T(8,128)(2,1)}), bf16[64,4,128]{2,0,1:T(8,128)(2,1)S(1)}, u32[]{:S(2)}, u32[]{:S(2)}) async-start(bf16[64,4,128]{2,0,1:T(8,128)(2,1)} %copy.71), calls=%async_computation | async-start | bytes 131072 | tf_op jit(solution)/shard_map/all_to_all | solution.py:69
  80.7 89.5 %all-gather.3.cloned.1.call-start = ((), (), s32[]{:S(2)}) async-start(), calls=%async_computation.2 | async-start | bytes 8650752 | tf_op jit(solution)/shard_map/all_gather | solution.py:79
  86.8 7.6 %all-to-all-start.1 = ((bf16[4,64,128]{2,1,0:T(8,128)(2,1)}), bf16[4,64,128]{2,1,0:T(8,128)(2,1)S(1)}, u32[]{:S(2)}, u32[]{:S(2)}) async-start(bf16[4,64,128]{2,1,0:T(8,128)(2,1)} %bitcast.31), calls=%async_computation.1 | async-start | bytes 131072 | tf_op jit(solution)/shard_map/all_to_all | solution.py:82
  95.9 10.9 %collective-permute-start.1 = (f32[64,4,128]{2,1,0:T(4,128)S(1)}, f32[64,4,128]{2,1,0:T(4,128)S(1)}, u32[]{:S(2)}, u32[]{:S(2)}) collective-permute-start(f32[64,4,128]{2,1,0:T(4,128)S(1)} %get-tuple-element.652), channel_id=1, source_target_pairs={{0,4},{4,8},{8,12},{12,16},{16,20},{20,24},{24,28},{28,0},{1,5},{5... | collective-permute-start | bytes 393224 | tf_op jit(solution)/shard_map/while/body/eval_jaxpr/ppermute | solution.py:9
  107.2 7.9 %collective-permute-start.1 = (f32[64,4,128]{2,1,0:T(4,128)S(1)}, f32[64,4,128]{2,1,0:T(4,128)S(1)}, u32[]{:S(2)}, u32[]{:S(2)}) collective-permute-start(f32[64,4,128]{2,1,0:T(4,128)S(1)} %get-tuple-element.652), channel_id=1, source_target_pairs={{0,4},{4,8},{8,12},{12,16},{16,20},{20,24},{24,28},{28,0},{1,5},{5... | collective-permute-start | bytes 393224 | tf_op jit(solution)/shard_map/while/body/eval_jaxpr/ppermute | solution.py:9
  115.4 9.5 %collective-permute-start.1 = (f32[64,4,128]{2,1,0:T(4,128)S(1)}, f32[64,4,128]{2,1,0:T(4,128)S(1)}, u32[]{:S(2)}, u32[]{:S(2)}) collective-permute-start(f32[64,4,128]{2,1,0:T(4,128)S(1)} %get-tuple-element.652), channel_id=1, source_target_pairs={{0,4},{4,8},{8,12},{12,16},{16,20},{20,24},{24,28},{28,0},{1,5},{5... | collective-permute-start | bytes 393224 | tf_op jit(solution)/shard_map/while/body/eval_jaxpr/ppermute | solution.py:9
  125.3 9.7 %collective-permute-start.1 = (f32[64,4,128]{2,1,0:T(4,128)S(1)}, f32[64,4,128]{2,1,0:T(4,128)S(1)}, u32[]{:S(2)}, u32[]{:S(2)}) collective-permute-start(f32[64,4,128]{2,1,0:T(4,128)S(1)} %get-tuple-element.652), channel_id=1, source_target_pairs={{0,4},{4,8},{8,12},{12,16},{16,20},{20,24},{24,28},{28,0},{1,5},{5... | collective-permute-start | bytes 393224 | tf_op jit(solution)/shard_map/while/body/eval_jaxpr/ppermute | solution.py:9
  135.4 10.5 %collective-permute-start.1 = (f32[64,4,128]{2,1,0:T(4,128)S(1)}, f32[64,4,128]{2,1,0:T(4,128)S(1)}, u32[]{:S(2)}, u32[]{:S(2)}) collective-permute-start(f32[64,4,128]{2,1,0:T(4,128)S(1)} %get-tuple-element.652), channel_id=1, source_target_pairs={{0,4},{4,8},{8,12},{12,16},{16,20},{20,24},{24,28},{28,0},{1,5},{5... | collective-permute-start | bytes 393224 | tf_op jit(solution)/shard_map/while/body/eval_jaxpr/ppermute | solution.py:9
  146.2 10.9 %collective-permute-start.1 = (f32[64,4,128]{2,1,0:T(4,128)S(1)}, f32[64,4,128]{2,1,0:T(4,128)S(1)}, u32[]{:S(2)}, u32[]{:S(2)}) collective-permute-start(f32[64,4,128]{2,1,0:T(4,128)S(1)} %get-tuple-element.652), channel_id=1, source_target_pairs={{0,4},{4,8},{8,12},{12,16},{16,20},{20,24},{24,28},{28,0},{1,5},{5... | collective-permute-start | bytes 393224 | tf_op jit(solution)/shard_map/while/body/eval_jaxpr/ppermute | solution.py:9
  157.5 10.3 %collective-permute-start.1 = (f32[64,4,128]{2,1,0:T(4,128)S(1)}, f32[64,4,128]{2,1,0:T(4,128)S(1)}, u32[]{:S(2)}, u32[]{:S(2)}) collective-permute-start(f32[64,4,128]{2,1,0:T(4,128)S(1)} %get-tuple-element.652), channel_id=1, source_target_pairs={{0,4},{4,8},{8,12},{12,16},{16,20},{20,24},{24,28},{28,0},{1,5},{5... | collective-permute-start | bytes 393224 | tf_op jit(solution)/shard_map/while/body/eval_jaxpr/ppermute | solution.py:9
Sparse Core Ops, SparseCore 0:
  86.0 84.1 all-gather.2
